TPU v7x, 32 devices: a whole 2x2x4 slice. The times are simulated.
32 devices in a mesh: groups: 2 (over y), blk: 4 (over z), rep: 2 (over x), sub: 2 (over core).
Axes of the slice: x: 2, y: 2, z: 4, core: 2. Of those that a mesh axis runs over, the one named last changes fastest.
Arguments:
- replica_delta: bfloat16 [32, 32, 4608], P(('groups', 'blk', 'rep', 'sub')), parts along dimension 0, may hold values from -150 to 150
- momentum: float32 [64, 4608], P(('groups', 'blk')), parts along dimension 0, may hold values from -6 to 6
- params: float32 [64, 4608], P(('groups', 'blk')), parts along dimension 0, may hold values from -6 to 6
- prev_master: float32 [64, 4608], P(('groups', 'blk')), parts along dimension 0, may hold values from -6 to 6
Outputs:
- new_params: float32 [64, 4608], P(('groups', 'blk')), parts along dimension 0
- new_momentum: float32 [64, 4608], P(('groups', 'blk')), parts along dimension 0
- prev_weights: bfloat16 [64, 4608], P('groups'), parts along dimension 0
There are 2 independent parts, one for each index of `groups`. A program takes and returns all parts, laid end to end along the dimension named above; each array names one. Nothing has to cross between parts.
All inputs are finite; a program needn't handle non-finite values.
Results may differ from a plain program's by a relative error of at most 0.012.
Values may be sent and summed in bfloat16 or wider, within the bound.
A program may use at most 64 MiB of HBM per device.

v0:
```python
import jax
import jax.numpy as jnp
from jax import lax
from jax.sharding import PartitionSpec as P

momentum_coef = 0.9
outer_rate = 0.7


def per_device(replica_delta, momentum, params, prev_master):
    own_delta = replica_delta[0]
    width = own_delta.shape[1]
    entries = own_delta.shape[0] * width
    share_sum = lax.psum_scatter(
        own_delta.astype(jnp.float32).astype(jnp.bfloat16), "blk", scatter_dimension=0, tiled=True
    )
    summed = lax.psum(share_sum, ("rep", "sub")).astype(jnp.float32)
    squares = lax.psum(jnp.sum(summed * summed), "blk")
    clip_factor = jnp.minimum(
        jnp.float32(1.0), jnp.sqrt(jnp.float32(entries)) / jnp.sqrt(squares + 1e-06)
    )
    scaled = clip_factor * summed
    new_momentum = momentum_coef * momentum + scaled
    new_params = params - outer_rate * (scaled + momentum_coef * new_momentum)
    prev_weights = lax.all_gather(prev_master.astype(jnp.bfloat16), "blk", axis=0, tiled=True)
    return (new_params, new_momentum, prev_weights)


def solution(mesh):
    in_specs = (
        P(("groups", "blk", "rep", "sub"), None, None),
        P(("groups", "blk"), None),
        P(("groups", "blk"), None),
        P(("groups", "blk"), None),
    )
    out_specs = (P(("groups", "blk"), None), P(("groups", "blk"), None), P("groups", None))
    return jax.shard_map(
        per_device, mesh=mesh, in_specs=in_specs, out_specs=out_specs, check_vma=False
    )
```

profile of v0, /device:TPU:0, one launch (start us, length us, event | category | flops | bytes accessed | tf_op | source)
XLA Modules:
  0.0 86.8 jit_solution(3447558341183904942)
XLA Ops:
  7.2 0.0 reduce-scatter.2.cloned.1.call-start
  7.2 0.0 copy-start.1
  7.2 0.7 reduce-scatter.2.cloned.1.call-update
  7.9 0.0 all-reduce.2.cloned.1.call-start
  7.9 0.2 copy-done.1
  8.1 25.1 %reduce-scatter.2.cloned.1.call-done = bf16[8,4608]{1,0:T(8,128)(2,1)} async-done(((bf16[32,4608]{1,0:T(8,128)(2,1)}), bf16[8,4608]{1,0:T(8,128)(2,1)}) %reduce-scatter.2.cloned.1.call-update) | async-done | bytes 73744 | tf_op jit(solution)/shard_map/reduce_scatter | solution.py:14
  33.2 0.0 all-reduce.2.cloned.1.call-update
  33.2 0.0 copy-start.2
  33.2 0.0 copy-start.3
  33.2 14.1 %all_gather.3 = bf16[32,4608]{1,0:T(8,128)(2,1)S(1)} all-gather(bf16[8,4608]{1,0:T(8,128)(2,1)S(1)} %convert_element_type.9), channel_id=1, replica_groups=mesh['groups'=2,'blk'=4,'rep'=2,'sub'=2] {'blk'}, dimensions={0}, use_global_device_ids=true | all-gather | bytes 368640 | tf_op jit(solution)/shard_map/all_gather | solution.py:25
  47.4 16.1 %all-reduce.2.cloned.1.call-done = bf16[8,4608]{1,0:T(8,128)(2,1)} async-done(((bf16[8,4608]{1,0:T(8,128)(2,1)}), bf16[8,4608]{1,0:T(8,128)(2,1)}) %all-reduce.2.cloned.1.call-update) | async-done | bytes 73744 | tf_op jit(solution)/shard_map/psum | solution.py:17
  63.5 0.0 copy-start
  63.5 1.6 %fusion.4 = f32[]{:T(128)} fusion(bf16[8,4608]{1,0:T(8,128)(2,1)} %all-reduce.2.cloned.1.call-done), kind=kLoop, calls=%fused_computation.6 | loop fusion | flops 110591 | bytes 73732 | tf_op jit(solution)/shard_map/reduce_sum | solution.py:18
  65.1 12.7 %psum.15 = f32[]{:T(128)} all-reduce(f32[]{:T(128)} %fusion.4), channel_id=1, replica_groups=mesh['groups'=2,'blk'=4,'rep'=2,'sub'=2] {'blk'}, use_global_device_ids=true, to_apply=%region_3.0 | all-reduce | flops 1 | bytes 8 | tf_op jit(solution)/shard_map/psum | solution.py:18
  78.4 0.0 copy-done.2
  78.5 0.0 copy-done.3
  78.5 0.0 copy-done
  78.5 0.8 fusion.3
  79.2 0.7 copy.9
  (1 shorter events, 0.0 us)
Async XLA Ops:
  7.2 26.0 %reduce-scatter.2.cloned.1.call-start = ((), (), s32[]{:S(2)}) async-start(), calls=%async_computation.1 | async-start | bytes 368640 | tf_op jit(solution)/shard_map/reduce_scatter | solution.py:14
  7.2 0.9 %copy-start.1 = (f32[8,4608]{1,0:T(8,128)S(1)}, f32[8,4608]{1,0:T(8,128)}, u32[]{:S(2)}) copy-start(f32[8,4608]{1,0:T(8,128)} %param.7) | copy-start | bytes 442372
  7.9 55.6 %all-reduce.2.cloned.1.call-start = ((), (), s32[]{:S(2)}) async-start(), calls=%async_computation.2 | async-start | bytes 147456 | tf_op jit(solution)/shard_map/psum | solution.py:17
  33.2 45.2 %copy-start.2 = (f32[8,4608]{1,0:T(8,128)S(1)}, f32[8,4608]{1,0:T(8,128)}, u32[]{:S(2)}) copy-start(f32[8,4608]{1,0:T(8,128)} %param.6) | copy-start | bytes 442372
  33.2 45.2 %copy-start.3 = (f32[8,4608]{1,0:T(8,128)S(1)}, f32[8,4608]{1,0:T(8,128)}, u32[]{:S(2)}) copy-start(f32[8,4608]{1,0:T(8,128)} %param.5) | copy-start | bytes 442372
  63.5 15.0 %copy-start = (bf16[8,4608]{1,0:T(8,128)(2,1)S(1)}, bf16[8,4608]{1,0:T(8,128)(2,1)}, u32[]{:S(2)}) copy-start(bf16[8,4608]{1,0:T(8,128)(2,1)} %all-reduce.2.cloned.1.call-done) | copy-start | bytes 221188
Sparse Core Ops, SparseCore 0:
  10.2 22.9 reduce-scatter.1
  35.5 27.9 all-reduce.1
where the time goes:
time: 87 us; the launch traced here: 86.8 us
  waiting for transfers between devices  41.9 us (48%)
  blocking collectives  26.8 us (31%)
  between operations  14.8 us (17%)
  other arithmetic  2.36 us (3%)
  local copies, waits for them, and re-layouts  0.91 us (1%)
    reduce_scatter x1, waiting for transfers between devices, per_device(): lax.psum_scatter(own_delta.astype(jnp.float32).astype(jnp.bfloat16), 'blk...  25.1 us
    psum x1, waiting for transfers between devices, per_device(): summed = lax.psum(share_sum, ('rep', 'sub')).astype(jnp.float32)  16.1 us
    all_gather x1, blocking collectives, per_device(): lax.all_gather(prev_master.astype(jnp.bfloat16), 'blk', axis=0, tiled=True)  14.1 us
    psum x1, blocking collectives, per_device(): squares = lax.psum(jnp.sum(summed * summed), 'blk')  12.7 us
  transfers between devices with their start and end apart: 2, of which 2 were waited for; matrix products, arithmetic and copies ran while one was open for 0% of the time, Pallas kernels for 0%

commit v1 on v0

--- a/solution.py
+++ b/solution.py
@@ -1,19 +1,232 @@
+import functools
+import itertools
+import math
+
 import jax
 import jax.numpy as jnp
 from jax import lax
+from jax.experimental import pallas as pl
+from jax.experimental.pallas import tpu as pltpu
 from jax.sharding import PartitionSpec as P
 
 momentum_coef = 0.9
 outer_rate = 0.7
-
-
-def per_device(replica_delta, momentum, params, prev_master):
+MESH = pl.DeviceIdType.MESH
+LANES = 128
+
+
+def flip(index, mask):
+    bit = 1
+    while bit <= mask:
+        if mask & bit:
+            index = index + bit * (1 - 2 * ((index // bit) % 2))
+        bit *= 2
+    return index
+
+
+def kernel(sizes, delta_hbm, mom_hbm, par_hbm, prev_hbm, new_par_hbm, new_mom_hbm, prev_out_hbm,
+           delta, mom, par, prev, recv1, half, mine, recv2, part, recv3, total, squares, weights, new_par, new_mom,
+           load_sem, store_sem, send1, got1, send2, got2, send3, got3, send_g, got_g, send_q, got_q,
+           send_pz, got_pz, send_px, got_px, send_pc, got_pc):
+    nz, nx, ns = sizes
+    z, x, s = lax.axis_index("blk"), lax.axis_index("rep"), lax.axis_index("sub")
+    own, width = mom.shape
+    half_width = width // ns
+    piece = half_width // nx
+
+    def columns(core, rep):
+        return pl.ds(pl.multiple_of(core * half_width + rep * piece, LANES), piece)
+
+    def half_columns(core):
+        return pl.ds(pl.multiple_of(core * half_width, LANES), half_width)
+
+    def inner(rep):
+        return pl.ds(pl.multiple_of(rep * piece, LANES), piece)
+
+    def peer(tz, tx, ts):
+        return {"blk": flip(z, tz), "rep": flip(x, tx), "sub": flip(s, ts)}
+
+    def remote(src, dst, send, got, to):
+        copy = pltpu.make_async_remote_copy(
+            src_ref=src, dst_ref=dst, send_sem=send, recv_sem=got, device_id=peer(*to), device_id_type=MESH
+        )
+        copy.start()
+        started.append(copy)
+        return copy
+
+    started = []
+    offsets = [o for o in itertools.product(range(nz), range(nx), range(ns)) if o != (0, 0, 0)]
+    barrier = pltpu.get_barrier_semaphore()
+    for o in offsets:
+        pl.semaphore_signal(barrier, inc=1, device_id=peer(*o), device_id_type=MESH)
+
+    loads = [
+        pltpu.make_async_copy(src, dst, load_sem.at[i])
+        for i, (src, dst) in enumerate(((prev_hbm, prev), (delta_hbm, delta), (mom_hbm, mom), (par_hbm, par)))
+    ]
+    for copy in loads:
+        copy.start()
+    loads[0].wait()
+    weights[z] = prev[...].astype(weights.dtype)
+    loads[1].wait()
+    pl.semaphore_wait(barrier, len(offsets))
+
+    order = list(range(nz - 1, -1, -1))
+    first = {
+        t: remote(delta.at[flip(z, t), :, half_columns(1 - s)], recv1.at[t], send1.at[t], got1.at[t], (0, 0, 1))
+        for t in order
+    }
+    across = {
+        t: remote(weights.at[z, :, columns(s, x)], weights.at[z, :, columns(s, x)], send_pz.at[t], got_pz.at[t], (t, 0, 0))
+        for t in order if t
+    }
+
+    second, third = {}, {}
+
+    def stage_two(t):
+        first[t].wait_recv()
+        zt = flip(z, t)
+        for u in range(nx - 1, 0, -1):
+            xu = flip(x, u)
+            half[t, u] = (
+                delta[zt, :, columns(s, xu)].astype(jnp.float32) + recv1[t, :, inner(xu)].astype(jnp.float32)
+            ).astype(half.dtype)
+            second[t, u] = remote(half.at[t, u], recv2.at[t, u], send2.at[t, u], got2.at[t, u], (0, u, 0))
+        mine[t] = delta[zt, :, columns(s, x)].astype(jnp.float32) + recv1[t, :, inner(x)].astype(jnp.float32)
+
+    def stage_three(t):
+        value = mine[t]
+        for u in range(1, nx):
+            second[t, u].wait_recv()
+            value = value + recv2[t, u].astype(jnp.float32)
+        if t:
+            part[t] = value.astype(part.dtype)
+            third[t] = remote(part.at[t], recv3.at[t], send3.at[t], got3.at[t], (t, 0, 0))
+        else:
+            mine[t] = value
+
+    for i, t in enumerate(order):
+        stage_two(t)
+        if i:
+            stage_three(order[i - 1])
+    stage_three(order[-1])
+
+    along = {}
+    for t in order:
+        if t:
+            across[t].wait_recv()
+            place = weights.at[flip(z, t), :, columns(s, x)]
+            for u in range(1, nx):
+                along[t, u] = remote(place, place, send_px.at[t, u], got_px.at[t, u], (0, u, 0))
+
+    value = mine[0]
+    for t in sorted(third):
+        third[t].wait_recv()
+        value = value + recv3[t].astype(jnp.float32)
+    rounded = value.astype(total.dtype)
+    total[:, columns(s, x)] = rounded
+    value = rounded.astype(jnp.float32)
+    square = jnp.sum(value * value, axis=0, keepdims=True)
+    lanes = square[:, :LANES]
+    for c in range(1, piece // LANES):
+        lanes = lanes + square[:, c * LANES : (c + 1) * LANES]
+    place = (z * nx + x) * ns + s
+    squares[place] = lanes
+    norms = [
+        remote(squares.at[place], squares.at[place], send_q.at[i], got_q.at[i], o)
+        for i, o in sorted(enumerate(offsets), key=lambda e: (-e[1][0], -e[1][1], -e[1][2]))
+    ]
+    sums = [
+        remote(total.at[:, columns(s, x)], total.at[:, columns(s, x)], send_g.at[u, c], got_g.at[u, c], (0, u, c))
+        for u in range(nx - 1, -1, -1) for c in range(ns - 1, -1, -1) if u or c
+    ]
+
+    over = {}
+    for t in order:
+        if t:
+            for u in range(1, nx):
+                along[t, u].wait_recv()
+            place = weights.at[flip(z, t), :, half_columns(s)]
+            over[t] = remote(place, place, send_pc.at[t], got_pc.at[t], (0, 0, 1))
+
+    loads[2].wait()
+    loads[3].wait()
+    for copy in sums:
+        copy.wait_recv()
+    for t in over:
+        over[t].wait_recv()
+    stores = [pltpu.make_async_copy(weights, prev_out_hbm, store_sem.at[0])]
+    stores[0].start()
+    for copy in norms:
+        copy.wait_recv()
+    norm = jnp.sum(jnp.sum(squares[...], axis=0), axis=1, keepdims=True)
+    limit = math.sqrt(nz * own * width)
+    clip = jnp.minimum(jnp.float32(1.0), jnp.float32(limit) / jnp.sqrt(norm + jnp.float32(1e-06)))
+    scaled = clip * total[...].astype(jnp.float32)
+    fresh = momentum_coef * mom[...] + scaled
+    new_mom[...] = fresh
+    stores.append(pltpu.make_async_copy(new_mom, new_mom_hbm, store_sem.at[1]))
+    stores[-1].start()
+    new_par[...] = par[...] - outer_rate * (scaled + momentum_coef * fresh)
+    stores.append(pltpu.make_async_copy(new_par, new_par_hbm, store_sem.at[2]))
+    stores[-1].start()
+    for copy in started:
+        copy.wait_send()
+    for copy in stores:
+        copy.wait()
+
+
+def by_kernel(sizes, replica_delta, momentum, params, prev_master):
+    nz, nx, ns = sizes
+    own, width = momentum.shape
+    half, piece = width // ns, width // (ns * nx)
+    b16, f32, dma = jnp.bfloat16, jnp.float32, pltpu.SemaphoreType.DMA
+    delta = replica_delta.reshape(nz, own, width)
+    any_space = pl.BlockSpec(memory_space=pl.ANY)
+    new_params, new_momentum, weights = pl.pallas_call(
+        functools.partial(kernel, sizes),
+        out_shape=(
+            jax.ShapeDtypeStruct((own, width), f32),
+            jax.ShapeDtypeStruct((own, width), f32),
+            jax.ShapeDtypeStruct((nz, own, width), b16),
+        ),
+        in_specs=[any_space] * 4,
+        out_specs=[any_space] * 3,
+        scratch_shapes=[
+            pltpu.VMEM((nz, own, width), b16),
+            pltpu.VMEM((own, width), f32),
+            pltpu.VMEM((own, width), f32),
+            pltpu.VMEM((own, width), f32),
+            pltpu.VMEM((nz, own, half), b16),
+            pltpu.VMEM((nz, nx, own, piece), b16),
+            pltpu.VMEM((nz, own, piece), f32),
+            pltpu.VMEM((nz, nx, own, piece), b16),
+            pltpu.VMEM((nz, own, piece), b16),
+            pltpu.VMEM((nz, own, piece), b16),
+            pltpu.VMEM((own, width), b16),
+            pltpu.VMEM((nz * nx * ns, 1, LANES), f32),
+            pltpu.VMEM((nz, own, width), b16),
+            pltpu.VMEM((own, width), f32),
+            pltpu.VMEM((own, width), f32),
+            dma((4,)), dma((3,)),
+            dma((nz,)), dma((nz,)),
+            dma((nz, nx)), dma((nz, nx)),
+            dma((nz,)), dma((nz,)),
+            dma((nx, ns)), dma((nx, ns)),
+            dma((nz * nx * ns,)), dma((nz * nx * ns,)),
+            dma((nz,)), dma((nz,)),
+            dma((nz, nx)), dma((nz, nx)),
+            dma((nz,)), dma((nz,)),
+        ],
+        compiler_params=pltpu.CompilerParams(collective_id=0, has_side_effects=True),
+    )(delta, momentum, params, prev_master)
+    return new_params, new_momentum, weights.reshape(nz * own, width)
+
+
+def by_collectives(replica_delta, momentum, params, prev_master):
     own_delta = replica_delta[0]
-    width = own_delta.shape[1]
-    entries = own_delta.shape[0] * width
-    share_sum = lax.psum_scatter(
-        own_delta.astype(jnp.float32).astype(jnp.bfloat16), "blk", scatter_dimension=0, tiled=True
-    )
+    entries = own_delta.shape[0] * own_delta.shape[1]
+    share_sum = lax.psum_scatter(own_delta, "blk", scatter_dimension=0, tiled=True)
     summed = lax.psum(share_sum, ("rep", "sub")).astype(jnp.float32)
     squares = lax.psum(jnp.sum(summed * summed), "blk")
     clip_factor = jnp.minimum(
@@ -27,6 +240,16 @@
 
 
 def solution(mesh):
+    sizes = tuple(mesh.shape[a] for a in ("blk", "rep", "sub"))
+
+    def per_device(replica_delta, momentum, params, prev_master):
+        width = momentum.shape[1]
+        whole_pieces = width % (LANES * sizes[1] * sizes[2]) == 0
+        powers = all(n & (n - 1) == 0 for n in sizes) and sizes[2] == 2
+        if whole_pieces and powers:
+            return by_kernel(sizes, replica_delta, momentum, params, prev_master)
+        return by_collectives(replica_delta, momentum, params, prev_master)
+
     in_specs = (
         P(("groups", "blk", "rep", "sub"), None, None),
         P(("groups", "blk"), None),

time: 87 us -> 23.7 us (0.27)
  waiting for transfers between devices: 41.9 us -> 0 us
  blocking collectives: 26.8 us -> 0 us
  Pallas kernels: 0 us -> 19.9 us
  between operations: 14.8 us -> 0.66 us
  other arithmetic: 2.36 us -> 0 us
  local copies, waits for them, and re-layouts: 0.91 us -> 3.02 us
    reduce_scatter x1 -> x0, waiting for transfers between devices: 25.1 us -> none  [per_device(): lax.psum_scatter(own_delta.astype(jnp.float32).astype(jnp.bfloat16), 'blk...]
    pallas_call x0 -> x1, Pallas kernels: none -> 19.9 us  [by_kernel(): pl.pallas_call(functools.partial(kernel, sizes), out_shape=(jax.ShapeDtyp...]
    psum x1 -> x0, waiting for transfers between devices: 16.1 us -> none  [per_device(): summed = lax.psum(share_sum, ('rep', 'sub')).astype(jnp.float32)]
    all_gather x1 -> x0, blocking collectives: 14.1 us -> none  [per_device(): lax.all_gather(prev_master.astype(jnp.bfloat16), 'blk', axis=0, tiled=True)]
    psum x1 -> x0, blocking collectives: 12.7 us -> none  [per_device(): squares = lax.psum(jnp.sum(summed * summed), 'blk')]
    unnamed x9 -> x7, local copies, waits for them, and re-layouts: 0.91 us -> 3.02 us
    reduce_sum x1 -> x0, other arithmetic: 1.6 us -> none  [per_device(): squares = lax.psum(jnp.sum(summed * summed), 'blk')]
  transfers between devices with their start and end apart: 2 -> 0, of which waited for: 2 -> 0; matrix products, arithmetic and copies ran while one was open for 0% -> 0% of each run, Pallas kernels for 0% -> 0%
where the time goes in v1:
time: 23.7 us; the launch traced here: 23.5 us
  Pallas kernels  19.9 us (84%)
  local copies, waits for them, and re-layouts  3.02 us (13%)
  between operations  0.66 us (3%)
    pallas_call x1, Pallas kernels, by_kernel(): pl.pallas_call(functools.partial(kernel, sizes), out_shape=(jax.ShapeDtyp...  19.9 us
    unnamed x7, local copies, waits for them, and re-layouts  3.02 us

profile of v1, /device:TPU:0, one launch (start us, length us, event | category | flops | bytes accessed | tf_op | source)
XLA Modules:
  0.0 23.5 jit_solution(10660452253123260991)
XLA Ops:
  0.6 19.9 %shard_map.67 = (f32[8,4608]{1,0:T(8,128)}, f32[8,4608]{1,0:T(8,128)}, bf16[4,8,4608]{2,1,0:T(8,128)(2,1)}) custom-call(bf16[4,8,4608]{2,1,0:T(8,128)(2,1)} %bitcast.3, f32[8,4608]{1,0:T(8,128)} %mom_hbm.1, f32[8,4608]{1,0:T(8,128)} %par_hbm.1, f32[8,4608]{1,0:T(8,128)} %prev_hbm.1), custom_call_target="tpu_custom_call" | custom-call | tf_op jit(solution)/shard_map/pallas_call | solution.py:186
  20.5 0.0 copy-start.1
  20.5 0.0 copy-start
  20.5 1.6 %copy.10 = f32[8,4608]{1,0:T(8,128)} copy(f32[8,4608]{1,0:T(8,128)} %get-tuple-element.12) | data formatting | bytes 294912
  22.1 0.0 copy-done.1
  22.1 0.7 %copy.11 = f32[8,4608]{1,0:T(8,128)} copy(f32[8,4608]{1,0:T(8,128)S(1)} %copy-done.1) | data formatting | bytes 294912
  22.8 0.0 copy-done
  22.8 0.7 %copy.12 = bf16[32,4608]{1,0:T(8,128)(2,1)} copy(bf16[32,4608]{1,0:T(8,128)(2,1)S(1)} %bitcast.2) | data formatting | bytes 589824
Async XLA Ops:
  20.5 1.7 %copy-start.1 = (f32[8,4608]{1,0:T(8,128)S(1)}, f32[8,4608]{1,0:T(8,128)}, u32[]{:S(2)}) copy-start(f32[8,4608]{1,0:T(8,128)} %get-tuple-element.13) | copy-start | bytes 442372
  20.5 2.3 %copy-start = (bf16[4,8,4608]{2,1,0:T(8,128)(2,1)S(1)}, bf16[4,8,4608]{2,1,0:T(8,128)(2,1)}, u32[]{:S(2)}) copy-start(bf16[4,8,4608]{2,1,0:T(8,128)(2,1)} %get-tuple-element.8) | copy-start | bytes 884740

commit v2 on v1

--- a/solution.py
+++ b/solution.py
@@ -24,10 +24,10 @@
     return index
 
 
-def kernel(sizes, delta_hbm, mom_hbm, par_hbm, prev_hbm, new_par_hbm, new_mom_hbm, prev_out_hbm,
-           delta, mom, par, prev, recv1, half, mine, recv2, part, recv3, total, squares, weights, new_par, new_mom,
-           load_sem, store_sem, send1, got1, send2, got2, send3, got3, send_g, got_g, send_q, got_q,
-           send_pz, got_pz, send_px, got_px, send_pc, got_pc):
+def exchange(sizes, delta_hbm, mom_hbm, par_hbm, prev_hbm, total, squares, weights, mom, par,
+             delta, prev, recv1, half, mine, recv2, part, recv3,
+             load_sem, send1, got1, send2, got2, send3, got3, send_g, got_g, send_q, got_q,
+             send_pz, got_pz, send_px, got_px, send_pc, got_pc):
     nz, nx, ns = sizes
     z, x, s = lax.axis_index("blk"), lax.axis_index("rep"), lax.axis_index("sub")
     own, width = mom.shape
@@ -151,16 +151,16 @@
 
     loads[2].wait()
     loads[3].wait()
-    for copy in sums:
+    for copy in sums + list(over.values()) + norms:
         copy.wait_recv()
-    for t in over:
-        over[t].wait_recv()
+    for copy in started:
+        copy.wait_send()
+
+
+def update(limit, total, squares, weights, mom, par, new_par_hbm, new_mom_hbm, prev_out_hbm, new_par, new_mom, store_sem):
     stores = [pltpu.make_async_copy(weights, prev_out_hbm, store_sem.at[0])]
     stores[0].start()
-    for copy in norms:
-        copy.wait_recv()
     norm = jnp.sum(jnp.sum(squares[...], axis=0), axis=1, keepdims=True)
-    limit = math.sqrt(nz * own * width)
     clip = jnp.minimum(jnp.float32(1.0), jnp.float32(limit) / jnp.sqrt(norm + jnp.float32(1e-06)))
     scaled = clip * total[...].astype(jnp.float32)
     fresh = momentum_coef * mom[...] + scaled
@@ -170,8 +170,6 @@
     new_par[...] = par[...] - outer_rate * (scaled + momentum_coef * fresh)
     stores.append(pltpu.make_async_copy(new_par, new_par_hbm, store_sem.at[2]))
     stores[-1].start()
-    for copy in started:
-        copy.wait_send()
     for copy in stores:
         copy.wait()
 
@@ -182,20 +180,20 @@
     half, piece = width // ns, width // (ns * nx)
     b16, f32, dma = jnp.bfloat16, jnp.float32, pltpu.SemaphoreType.DMA
     delta = replica_delta.reshape(nz, own, width)
-    any_space = pl.BlockSpec(memory_space=pl.ANY)
-    new_params, new_momentum, weights = pl.pallas_call(
-        functools.partial(kernel, sizes),
+    hbm_space, vmem_space = (pl.BlockSpec(memory_space=m) for m in (pltpu.HBM, pltpu.VMEM))
+    held = pl.pallas_call(
+        functools.partial(exchange, sizes),
         out_shape=(
-            jax.ShapeDtypeStruct((own, width), f32),
-            jax.ShapeDtypeStruct((own, width), f32),
-            jax.ShapeDtypeStruct((nz, own, width), b16),
-        ),
-        in_specs=[any_space] * 4,
-        out_specs=[any_space] * 3,
-        scratch_shapes=[
+            pltpu.VMEM((own, width), b16),
+            pltpu.VMEM((nz * nx * ns, 1, LANES), f32),
             pltpu.VMEM((nz, own, width), b16),
             pltpu.VMEM((own, width), f32),
             pltpu.VMEM((own, width), f32),
+        ),
+        in_specs=[hbm_space] * 4,
+        out_specs=[vmem_space] * 5,
+        scratch_shapes=[
+            pltpu.VMEM((nz, own, width), b16),
             pltpu.VMEM((own, width), f32),
             pltpu.VMEM((nz, own, half), b16),
             pltpu.VMEM((nz, nx, own, piece), b16),
@@ -203,12 +201,7 @@
             pltpu.VMEM((nz, nx, own, piece), b16),
             pltpu.VMEM((nz, own, piece), b16),
             pltpu.VMEM((nz, own, piece), b16),
-            pltpu.VMEM((own, width), b16),
-            pltpu.VMEM((nz * nx * ns, 1, LANES), f32),
-            pltpu.VMEM((nz, own, width), b16),
-            pltpu.VMEM((own, width), f32),
-            pltpu.VMEM((own, width), f32),
-            dma((4,)), dma((3,)),
+            dma((4,)),
             dma((nz,)), dma((nz,)),
             dma((nz, nx)), dma((nz, nx)),
             dma((nz,)), dma((nz,)),
@@ -218,8 +211,22 @@
             dma((nz, nx)), dma((nz, nx)),
             dma((nz,)), dma((nz,)),
         ],
-        compiler_params=pltpu.CompilerParams(collective_id=0, has_side_effects=True),
-    )(delta, momentum, params, prev_master)
+        compiler_params=pltpu.CompilerParams(
+            collective_id=0, has_side_effects=True, vmem_limit_bytes=16 * 1024 * 1024
+        ),
+    )(*(pltpu.with_memory_space_constraint(a, pltpu.HBM) for a in (delta, momentum, params, prev_master)))
+    new_params, new_momentum, weights = pl.pallas_call(
+        functools.partial(update, math.sqrt(nz * own * width)),
+        out_shape=(
+            jax.ShapeDtypeStruct((own, width), f32),
+            jax.ShapeDtypeStruct((own, width), f32),
+            jax.ShapeDtypeStruct((nz, own, width), b16),
+        ),
+        in_specs=[vmem_space] * 5,
+        out_specs=[hbm_space] * 3,
+        scratch_shapes=[pltpu.VMEM((own, width), f32), pltpu.VMEM((own, width), f32), dma((3,))],
+        compiler_params=pltpu.CompilerParams(vmem_limit_bytes=16 * 1024 * 1024),
+    )(*held)
     return new_params, new_momentum, weights.reshape(nz * own, width)
 
 

time: 23.7 us -> 20.7 us (0.87)
  local copies, waits for them, and re-layouts: 3.02 us -> 0 us
    unnamed x7 -> x0, local copies, waits for them, and re-layouts: 3.02 us -> none
    pallas_call x1 -> x2, Pallas kernels: 19.9 us -> 19.9 us  [the longest x1 19.1 us: by_kernel(): pl.pallas_call(functools.partial(exchange, sizes), out_shape=(pltpu.VMEM(...]
where the time goes in v2:
time: 20.7 us; the launch traced here: 20.6 us
  Pallas kernels  19.9 us (96%)
  between operations  0.64 us (3%)
    pallas_call x1, Pallas kernels, by_kernel(): pl.pallas_call(functools.partial(exchange, sizes), out_shape=(pltpu.VMEM(...  19.1 us
    pallas_call x1, Pallas kernels, by_kernel(): pl.pallas_call(functools.partial(update, math.sqrt(nz * own * width)), ou...  0.87 us

profile of v2, /device:TPU:0, one launch (start us, length us, event | category | flops | bytes accessed | tf_op | source)
XLA Modules:
  0.0 20.6 jit_solution(8169917918930855626)
XLA Ops:
  0.6 19.1 %shard_map.67 = (bf16[8,4608]{1,0:T(8,128)(2,1)S(1)}, f32[16,1,128]{2,1,0:T(1,128)S(1)}, bf16[4,8,4608]{2,1,0:T(8,128)(2,1)S(1)}, f32[8,4608]{1,0:T(8,128)S(1)}, f32[8,4608]{1,0:T(8,128)S(1)}) custom-call(bf16[4,8,4608]{2,1,0:T(8,128)(2,1)} %bitcast.2, f32[8,4608]{1,0:T(8,128)} %mom_hbm.1, f32[8,4608]{1,0:T(8,128)} %par_hbm.1, f32[8,4608]{1,0:T(8,128)} %prev_hbm.1), custom_call_target="tpu_custom_call" | custom-call | tf_op jit(solution)/shard_map/pallas_call | solution.py:184
  19.7 0.9 %shard_map.68 = (f32[8,4608]{1,0:T(8,128)}, f32[8,4608]{1,0:T(8,128)}, bf16[4,8,4608]{2,1,0:T(8,128)(2,1)}) custom-call(bf16[8,4608]{1,0:T(8,128)(2,1)S(1)} %get-tuple-element.11.total, f32[16,1,128]{2,1,0:T(1,128)S(1)} %get-tuple-element.12.squares, bf16[4,8,4608]{2,1,0:T(8,128)(2,1)S(1)} %get-tuple-element.13.weights, ...), custom_call_target="tpu_custom_call" | custom-call | tf_op jit(solution)/shard_map/pallas_call | solution.py:218

commit v3 on v2

--- a/solution.py
+++ b/solution.py
@@ -27,7 +27,7 @@
 def exchange(sizes, delta_hbm, mom_hbm, par_hbm, prev_hbm, total, squares, weights, mom, par,
              delta, prev, recv1, half, mine, recv2, part, recv3,
              load_sem, send1, got1, send2, got2, send3, got3, send_g, got_g, send_q, got_q,
-             send_pz, got_pz, send_px, got_px, send_pc, got_pc):
+             send_pz, got_pz, send_px, got_px, send_pc, got_pc, round_sem):
     nz, nx, ns = sizes
     z, x, s = lax.axis_index("blk"), lax.axis_index("rep"), lax.axis_index("sub")
     own, width = mom.shape
@@ -57,7 +57,20 @@
     started = []
     offsets = [o for o in itertools.product(range(nz), range(nx), range(ns)) if o != (0, 0, 0)]
     barrier = pltpu.get_barrier_semaphore()
-    for o in offsets:
+    around = (z > 0).astype(jnp.int32) + (z < nz - 1).astype(jnp.int32)
+
+    def greet(semaphore):
+        @pl.when(z > 0)
+        def _():
+            pl.semaphore_signal(semaphore, inc=1, device_id={"blk": z - 1}, device_id_type=MESH)
+
+        @pl.when(z < nz - 1)
+        def _():
+            pl.semaphore_signal(semaphore, inc=1, device_id={"blk": z + 1}, device_id_type=MESH)
+
+    greet(barrier)
+    near = [(0, u, 0) for u in range(1, nx)] + [(0, 0, c) for c in range(1, ns)]
+    for o in near:
         pl.semaphore_signal(barrier, inc=1, device_id=peer(*o), device_id_type=MESH)
 
     loads = [
@@ -69,18 +82,13 @@
     loads[0].wait()
     weights[z] = prev[...].astype(weights.dtype)
     loads[1].wait()
-    pl.semaphore_wait(barrier, len(offsets))
+    pl.semaphore_wait(barrier, around + len(near))
 
     order = list(range(nz - 1, -1, -1))
     first = {
         t: remote(delta.at[flip(z, t), :, half_columns(1 - s)], recv1.at[t], send1.at[t], got1.at[t], (0, 0, 1))
         for t in order
     }
-    across = {
-        t: remote(weights.at[z, :, columns(s, x)], weights.at[z, :, columns(s, x)], send_pz.at[t], got_pz.at[t], (t, 0, 0))
-        for t in order if t
-    }
-
     second, third = {}, {}
 
     def stage_two(t):
@@ -105,10 +113,25 @@
         else:
             mine[t] = value
 
-    for i, t in enumerate(order):
-        stage_two(t)
-        if i:
-            stage_three(order[i - 1])
+    if nz > 2:
+        greet(round_sem.at[0])
+    stage_two(order[0])
+    for r in range(nz - 2):
+        pl.semaphore_wait(round_sem.at[r], around)
+        if r + 1 < nz - 2:
+            greet(round_sem.at[r + 1])
+        if r == 0:
+            stage_two(order[1])
+    if nz == 2:
+        stage_two(order[1])
+    across = {
+        t: remote(weights.at[z, :, columns(s, x)], weights.at[z, :, columns(s, x)], send_pz.at[t], got_pz.at[t], (t, 0, 0))
+        for t in order if t
+    }
+    for i in range(1, nz):
+        stage_three(order[i - 1])
+        if i + 1 < nz:
+            stage_two(order[i + 1])
     stage_three(order[-1])
 
     along = {}
@@ -210,6 +233,7 @@
             dma((nz,)), dma((nz,)),
             dma((nz, nx)), dma((nz, nx)),
             dma((nz,)), dma((nz,)),
+            pltpu.SemaphoreType.REGULAR((max(nz - 2, 1),)),
         ],
         compiler_params=pltpu.CompilerParams(
             collective_id=0, has_side_effects=True, vmem_limit_bytes=16 * 1024 * 1024
@@ -252,7 +276,7 @@
     def per_device(replica_delta, momentum, params, prev_master):
         width = momentum.shape[1]
         whole_pieces = width % (LANES * sizes[1] * sizes[2]) == 0
-        powers = all(n & (n - 1) == 0 for n in sizes) and sizes[2] == 2
+        powers = all(n & (n - 1) == 0 and n > 1 for n in sizes) and sizes[2] == 2
         if whole_pieces and powers:
             return by_kernel(sizes, replica_delta, momentum, params, prev_master)
         return by_collectives(replica_delta, momentum, params, prev_master)

time: 20.7 us -> 20 us (0.966)
  Pallas kernels: 19.9 us -> 19.2 us
    pallas_call x1, Pallas kernels: 19.1 us -> 18.3 us  [by_kernel(): pl.pallas_call(functools.partial(exchange, sizes), out_shape=(pltpu.VMEM(...]
where the time goes in v3:
time: 20 us; the launch traced here: 19.8 us
  Pallas kernels  19.2 us (96%)
  between operations  0.64 us (3%)
    pallas_call x1, Pallas kernels, by_kernel(): pl.pallas_call(functools.partial(exchange, sizes), out_shape=(pltpu.VMEM(...  18.3 us
    pallas_call x1, Pallas kernels, by_kernel(): pl.pallas_call(functools.partial(update, math.sqrt(nz * own * width)), ou...  0.87 us

profile of v3, /device:TPU:0, one launch (start us, length us, event | category | flops | bytes accessed | tf_op | source)
XLA Modules:
  0.0 19.8 jit_solution(13442369743223695234)
XLA Ops:
  0.6 18.3 %shard_map.67 = (bf16[8,4608]{1,0:T(8,128)(2,1)S(1)}, f32[16,1,128]{2,1,0:T(1,128)S(1)}, bf16[4,8,4608]{2,1,0:T(8,128)(2,1)S(1)}, f32[8,4608]{1,0:T(8,128)S(1)}, f32[8,4608]{1,0:T(8,128)S(1)}) custom-call(bf16[4,8,4608]{2,1,0:T(8,128)(2,1)} %bitcast.2, f32[8,4608]{1,0:T(8,128)} %mom_hbm.1, f32[8,4608]{1,0:T(8,128)} %par_hbm.1, f32[8,4608]{1,0:T(8,128)} %prev_hbm.1), custom_call_target="tpu_custom_call" | custom-call | tf_op jit(solution)/shard_map/pallas_call | solution.py:207
  19.0 0.9 %shard_map.68 = (f32[8,4608]{1,0:T(8,128)}, f32[8,4608]{1,0:T(8,128)}, bf16[4,8,4608]{2,1,0:T(8,128)(2,1)}) custom-call(bf16[8,4608]{1,0:T(8,128)(2,1)S(1)} %get-tuple-element.11.total, f32[16,1,128]{2,1,0:T(1,128)S(1)} %get-tuple-element.12.squares, bf16[4,8,4608]{2,1,0:T(8,128)(2,1)S(1)} %get-tuple-element.13.weights, ...), custom_call_target="tpu_custom_call" | custom-call | tf_op jit(solution)/shard_map/pallas_call | solution.py:242

commit v4 on v3

--- a/solution.py
+++ b/solution.py
@@ -113,34 +113,32 @@
         else:
             mine[t] = value
 
+    across = {}
+
+    def send_previous(t):
+        place = weights.at[z, :, columns(s, x)]
+        across[t] = remote(place, place, send_pz.at[t], got_pz.at[t], (t, 0, 0))
+
     if nz > 2:
         greet(round_sem.at[0])
-    stage_two(order[0])
+    send_previous(1)
+    for t in order:
+        stage_two(t)
     for r in range(nz - 2):
         pl.semaphore_wait(round_sem.at[r], around)
         if r + 1 < nz - 2:
             greet(round_sem.at[r + 1])
-        if r == 0:
-            stage_two(order[1])
-    if nz == 2:
-        stage_two(order[1])
-    across = {
-        t: remote(weights.at[z, :, columns(s, x)], weights.at[z, :, columns(s, x)], send_pz.at[t], got_pz.at[t], (t, 0, 0))
-        for t in order if t
-    }
-    for i in range(1, nz):
-        stage_three(order[i - 1])
-        if i + 1 < nz:
-            stage_two(order[i + 1])
-    stage_three(order[-1])
-
-    along = {}
+        send_previous(r + 2)
     for t in order:
-        if t:
-            across[t].wait_recv()
-            place = weights.at[flip(z, t), :, columns(s, x)]
-            for u in range(1, nx):
-                along[t, u] = remote(place, place, send_px.at[t, u], got_px.at[t, u], (0, u, 0))
+        stage_three(t)
+
+    along, over = {}, []
+    for t in range(1, nz):
+        across[t].wait_recv()
+        place = weights.at[flip(z, t), :, columns(s, x)]
+        for u in range(1, nx):
+            along[t, u] = remote(place, place, send_px.at[t, u], got_px.at[t, u], (0, u, 0))
+        over.append(remote(place, place, send_pc.at[t, 0], got_pc.at[t, 0], (0, 0, 1)))
 
     value = mine[0]
     for t in sorted(third):
@@ -164,17 +162,14 @@
         for u in range(nx - 1, -1, -1) for c in range(ns - 1, -1, -1) if u or c
     ]
 
-    over = {}
-    for t in order:
-        if t:
-            for u in range(1, nx):
-                along[t, u].wait_recv()
-            place = weights.at[flip(z, t), :, half_columns(s)]
-            over[t] = remote(place, place, send_pc.at[t], got_pc.at[t], (0, 0, 1))
+    for (t, u), copy in along.items():
+        copy.wait_recv()
+        place = weights.at[flip(z, t), :, columns(s, flip(x, u))]
+        over.append(remote(place, place, send_pc.at[t, u], got_pc.at[t, u], (0, 0, 1)))
 
     loads[2].wait()
     loads[3].wait()
-    for copy in sums + list(over.values()) + norms:
+    for copy in sums + over + norms:
         copy.wait_recv()
     for copy in started:
         copy.wait_send()
@@ -232,7 +227,7 @@
             dma((nz * nx * ns,)), dma((nz * nx * ns,)),
             dma((nz,)), dma((nz,)),
             dma((nz, nx)), dma((nz, nx)),
-            dma((nz,)), dma((nz,)),
+            dma((nz, nx)), dma((nz, nx)),
             pltpu.SemaphoreType.REGULAR((max(nz - 2, 1),)),
         ],
         compiler_params=pltpu.CompilerParams(

time: 20 us -> 18.2 us (0.910)
  Pallas kernels: 19.2 us -> 17.4 us
    pallas_call x1, Pallas kernels: 18.3 us -> 16.5 us  [by_kernel(): pl.pallas_call(functools.partial(exchange, sizes), out_shape=(pltpu.VMEM(...]
where the time goes in v4:
time: 18.2 us; the launch traced here: 18 us
  Pallas kernels  17.4 us (96%)
  between operations  0.64 us (4%)
    pallas_call x1, Pallas kernels, by_kernel(): pl.pallas_call(functools.partial(exchange, sizes), out_shape=(pltpu.VMEM(...  16.5 us
    pallas_call x1, Pallas kernels, by_kernel(): pl.pallas_call(functools.partial(update, math.sqrt(nz * own * width)), ou...  0.87 us

profile of v4, /device:TPU:0, one launch (start us, length us, event | category | flops | bytes accessed | tf_op | source)
XLA Modules:
  0.0 18.0 jit_solution(9688265879531137296)
XLA Ops:
  0.6 16.5 %shard_map.67 = (bf16[8,4608]{1,0:T(8,128)(2,1)S(1)}, f32[16,1,128]{2,1,0:T(1,128)S(1)}, bf16[4,8,4608]{2,1,0:T(8,128)(2,1)S(1)}, f32[8,4608]{1,0:T(8,128)S(1)}, f32[8,4608]{1,0:T(8,128)S(1)}) custom-call(bf16[4,8,4608]{2,1,0:T(8,128)(2,1)} %bitcast.2, f32[8,4608]{1,0:T(8,128)} %mom_hbm.1, f32[8,4608]{1,0:T(8,128)} %par_hbm.1, f32[8,4608]{1,0:T(8,128)} %prev_hbm.1), custom_call_target="tpu_custom_call" | custom-call | tf_op jit(solution)/shard_map/pallas_call | solution.py:202
  17.1 0.9 %shard_map.68 = (f32[8,4608]{1,0:T(8,128)}, f32[8,4608]{1,0:T(8,128)}, bf16[4,8,4608]{2,1,0:T(8,128)(2,1)}) custom-call(bf16[8,4608]{1,0:T(8,128)(2,1)S(1)} %get-tuple-element.11.total, f32[16,1,128]{2,1,0:T(1,128)S(1)} %get-tuple-element.12.squares, bf16[4,8,4608]{2,1,0:T(8,128)(2,1)S(1)} %get-tuple-element.13.weights, ...), custom_call_target="tpu_custom_call" | custom-call | tf_op jit(solution)/shard_map/pallas_call | solution.py:237

commit v5 on v4

--- a/solution.py
+++ b/solution.py
@@ -75,13 +75,11 @@
 
     loads = [
         pltpu.make_async_copy(src, dst, load_sem.at[i])
-        for i, (src, dst) in enumerate(((prev_hbm, prev), (delta_hbm, delta), (mom_hbm, mom), (par_hbm, par)))
+        for i, (src, dst) in enumerate(((delta_hbm, delta), (prev_hbm, prev), (mom_hbm, mom), (par_hbm, par)))
     ]
     for copy in loads:
         copy.start()
     loads[0].wait()
-    weights[z] = prev[...].astype(weights.dtype)
-    loads[1].wait()
     pl.semaphore_wait(barrier, around + len(near))
 
     order = list(range(nz - 1, -1, -1))
@@ -121,6 +119,8 @@
 
     if nz > 2:
         greet(round_sem.at[0])
+    loads[1].wait()
+    weights[z] = prev[...].astype(weights.dtype)
     send_previous(1)
     for t in order:
         stage_two(t)

time: 18.2 us -> 18.2 us (level)
  no operation moved by 1% of the time
where the time goes in v5:
time: 18.2 us; the launch traced here: 18 us
  Pallas kernels  17.4 us (96%)
  between operations  0.64 us (4%)
    pallas_call x1, Pallas kernels, by_kernel(): pl.pallas_call(functools.partial(exchange, sizes), out_shape=(pltpu.VMEM(...  16.5 us
    pallas_call x1, Pallas kernels, by_kernel(): pl.pallas_call(functools.partial(update, math.sqrt(nz * own * width)), ou...  0.87 us

profile of v5, /device:TPU:0, one launch (start us, length us, event | category | flops | bytes accessed | tf_op | source)
XLA Modules:
  0.0 18.0 jit_solution(17305994119266396210)
XLA Ops:
  0.6 16.5 %shard_map.67 = (bf16[8,4608]{1,0:T(8,128)(2,1)S(1)}, f32[16,1,128]{2,1,0:T(1,128)S(1)}, bf16[4,8,4608]{2,1,0:T(8,128)(2,1)S(1)}, f32[8,4608]{1,0:T(8,128)S(1)}, f32[8,4608]{1,0:T(8,128)S(1)}) custom-call(bf16[4,8,4608]{2,1,0:T(8,128)(2,1)} %bitcast.2, f32[8,4608]{1,0:T(8,128)} %mom_hbm.1, f32[8,4608]{1,0:T(8,128)} %par_hbm.1, f32[8,4608]{1,0:T(8,128)} %prev_hbm.1), custom_call_target="tpu_custom_call" | custom-call | tf_op jit(solution)/shard_map/pallas_call | solution.py:202
  17.1 0.9 %shard_map.68 = (f32[8,4608]{1,0:T(8,128)}, f32[8,4608]{1,0:T(8,128)}, bf16[4,8,4608]{2,1,0:T(8,128)(2,1)}) custom-call(bf16[8,4608]{1,0:T(8,128)(2,1)S(1)} %get-tuple-element.11.total, f32[16,1,128]{2,1,0:T(1,128)S(1)} %get-tuple-element.12.squares, bf16[4,8,4608]{2,1,0:T(8,128)(2,1)S(1)} %get-tuple-element.13.weights, ...), custom_call_target="tpu_custom_call" | custom-call | tf_op jit(solution)/shard_map/pallas_call | solution.py:237
